TPU v7x, 512 devices: a whole 4x4x16 slice. The times are simulated.
512 devices in a mesh: section: 8 (over y_hi, x), head: 4 (over y_lo, core), tok: 16 (over z).
Axes of the slice: x: 4, y: 4 (y_hi: 2, y_lo: 2; y = y_hi * 2 + y_lo), z: 16, core: 2. Of those that a mesh axis runs over, the one named last changes fastest.
Arguments:
- held_cotangents: bfloat16 [8, 2, 2048, 2560], P('section', None, 'tok', 'head'), may hold values from -6 to 6
- entering_adjoint: bfloat16 [2048, 2560], P('tok', 'head'), may hold values from -6 to 6
- saved_queries: bfloat16 [8, 2048, 2560], P('section', 'tok', 'head'), may hold values from -1024 to 1024
- saved_keys: bfloat16 [8, 2048, 2560], P('section', 'tok', 'head'), may hold values from -20 to 20
- value_weight: bfloat16 [8, 2560, 2560], P('section', None, 'head'), may hold values from -0.125 to 0.125
- out_weight: bfloat16 [8, 2560, 2560], P('section', 'tok', 'head'), may hold values from -0.125 to 0.125
- block_gate: float32 [8, 2560], P('section'), may hold values from -3 to 3
- time_gate: float32 [32, 2560], replicated, may hold values from -3 to 3
- timestep: int32 [1], replicated, may hold values from 0 to 31
Outputs:
- passed: bfloat16 [8, 2, 2048, 2560], P('section', None, 'tok', 'head')
All inputs are finite; a program needn't handle non-finite values.
Results may differ from a plain program's by a relative error of at most 0.0085.
Values may be sent and summed in bfloat16 or wider, within the bound.
A program may use at most 64 MiB of HBM per device.

v0:
```python
import jax
import jax.numpy as jnp
from jax import lax
from jax.sharding import PartitionSpec as P

HD = 128


GUIDE = 3.0


def shifted(value, axis, steps):
    count = lax.axis_size(axis)
    leading, last = (max(0, -steps), min(count, count - steps))
    return lax.ppermute(value, axis, [(source, source + steps) for source in range(leading, last)])


def shards(
    held_cotangents,
    entering_adjoint,
    saved_queries,
    saved_keys,
    value_weight,
    out_weight,
    block_gate,
    time_gate,
    timestep,
):
    steps_index = jnp.arange(time_gate.shape[0])
    time_row = jnp.sum(
        jnp.where((steps_index == timestep[0])[:, None], time_gate, jnp.zeros_like(time_gate)),
        axis=0,
    )
    gate_row = block_gate[0] + time_row
    whole_cot = lax.all_gather(held_cotangents[0], "head", axis=2, tiled=True)
    scaled = (whole_cot.astype(jnp.float32) * gate_row).astype(jnp.bfloat16)
    out_full = lax.all_gather(out_weight[0], "tok", axis=0, tiled=True)
    attn_grad = jnp.einsum(
        "btd,dk->btk", scaled, out_full, preferred_element_type=jnp.float32
    ).astype(jnp.bfloat16)
    rows_here = saved_queries.shape[1]
    groups_here = saved_queries.shape[2] // HD
    score_scale = HD ** (-0.5)
    normal_grad = attn_grad[0]
    key_all = lax.all_gather(saved_keys[0], "tok", axis=0, tiled=True)
    key_heads = key_all.reshape(key_all.shape[0], groups_here, HD)
    query_heads = saved_queries[0].reshape(rows_here, groups_here, HD)
    scores = (
        jnp.einsum("ihe,jhe->hij", query_heads, key_heads, preferred_element_type=jnp.float32)
        * score_scale
    )
    row_top = jnp.max(scores, axis=2, keepdims=True)
    log_total = row_top + jnp.log(jnp.sum(jnp.exp(scores - row_top), axis=2, keepdims=True))
    weights = jnp.exp(scores - log_total).astype(jnp.bfloat16)
    grad_heads = normal_grad.reshape(rows_here, groups_here, HD)
    terms = jnp.einsum("hij,ihe->jhe", weights, grad_heads, preferred_element_type=jnp.float32)
    value_grad = lax.psum_scatter(
        terms.reshape(lax.axis_size("tok") * rows_here, groups_here * HD).astype(jnp.bfloat16),
        "tok",
        scatter_dimension=0,
        tiled=True,
    )
    stacked = jnp.stack([value_grad, attn_grad[1]])
    partial_back = jnp.einsum(
        "btk,dk->btd", stacked, value_weight[0], preferred_element_type=jnp.float32
    )
    back_sum = lax.psum_scatter(
        partial_back.astype(jnp.bfloat16), "head", scatter_dimension=2, tiled=True
    ).astype(jnp.float32)
    block_cot = (held_cotangents[0].astype(jnp.float32) + back_sum).astype(jnp.bfloat16)
    passed_on = shifted(block_cot, "section", -1)
    entering_full = entering_adjoint.astype(jnp.float32)
    fresh_rows = jnp.stack([(1.0 + GUIDE) * entering_full, -GUIDE * entering_full]).astype(
        jnp.bfloat16
    )
    is_last = lax.axis_index("section") == lax.axis_size("section") - 1
    return jnp.where(is_last, fresh_rows, passed_on)[None]


def solution(mesh):
    return jax.shard_map(
        shards,
        mesh=mesh,
        in_specs=(
            P("section", None, "tok", "head"),
            P("tok", "head"),
            P("section", "tok", "head"),
            P("section", "tok", "head"),
            P("section", None, "head"),
            P("section", "tok", "head"),
            P("section", None),
            P(),
            P(),
        ),
        out_specs=P("section", None, "tok", "head"),
        check_vma=False,
    )
```

profile of v0, /device:TPU:6, one launch (start us, length us, event | category | flops | bytes accessed | tf_op | source)
XLA Modules:
  0.0 357.0 jit_solution(16926532515218221262)
XLA Ops:
  6.5 0.0 copy-start
  6.5 0.0 all-gather.11.cloned.1.call-start
  6.5 1.9 copy.21
  8.4 0.0 all-gather.11.cloned.1.call-update
  8.4 0.0 all-gather.7.cloned.1.call-start
  8.5 0.7 all-gather.7.cloned.1.call-update
  9.2 0.0 all-gather.9.cloned.1.call-start
  9.2 0.7 all-gather.9.cloned.1.call-update
  9.9 0.0 reduce-scatter.5.cloned.1.call-start
  10.6 1.1 copy.20
  11.7 0.7 reduce
  12.4 1.1 select_reduce_fusion
  13.5 83.0 %all-gather.11.cloned.1.call-done = bf16[1,2048,640]{1,2,0:T(8,128)(2,1)} async-done(((bf16[1,128,640]{1,2,0:T(8,128)(2,1)}), bf16[1,2048,640]{1,2,0:T(8,128)(2,1)}) %all-gather.11.cloned.1.call-update) | async-done | bytes 2621456 | tf_op jit(solution)/shard_map/all_gather | solution.py:45
  96.6 2.7 multiply_reduce_fusion
  99.3 0.0 copy-start.1
  99.3 2.3 copy-done.1
  101.6 1.0 exponential_reduce_fusion
  102.6 21.9 %all-gather.7.cloned.1.call-done = bf16[1,2,128,2560]{3,2,1,0:T(8,128)(2,1)} async-done(((bf16[1,2,128,640]{3,2,1,0:T(8,128)(2,1)}), bf16[1,2,128,2560]{3,2,1,0:T(8,128)(2,1)}) %all-gather.7.cloned.1.call-update) | async-done | bytes 1310736 | tf_op jit(solution)/shard_map/all_gather | solution.py:35
  124.5 79.6 %all-gather.9.cloned.1.call-done = bf16[1,2560,640]{2,1,0:T(8,128)(2,1)} async-done(((bf16[1,160,640]{2,1,0:T(8,128)(2,1)}), bf16[1,2560,640]{2,1,0:T(8,128)(2,1)}) %all-gather.9.cloned.1.call-update) | async-done | bytes 3276816 | tf_op jit(solution)/shard_map/all_gather | solution.py:37
  204.2 3.5 fusion.9
  207.7 0.7 fusion.25
  208.4 0.8 copy.19
  209.2 5.3 %convolution_convert_fusion.1 = bf16[5,128,2048]{2,1,0:T(8,128)(2,1)} fusion(bf16[128,5,128]{0,2,1:T(8,128)(2,1)} %bitcast.51, f32[5,128,2048]{2,1,0:T(8,128)} %copy-done.1, f32[5,128]{1,0:T(8,128)S(1)} %log_add_fusion), kind=kOutput, calls=%fused_computation.7 | convolution fusion | flops 340787200 | bytes 8030720 | tf_op jit(solution)/shard_map/hij,ihe->jhe/dot_general | solution.py:56
  214.5 0.0 copy-start.2
  214.5 4.4 %copy.24 = bf16[2048,640]{1,0:T(8,128)(2,1)} copy(bf16[2048,640]{0,1:T(8,128)(2,1)} %bitcast.45) | data formatting | bytes 5242880 | tf_op jit(solution)/shard_map/convert_element_type | solution.py:58
  218.9 0.0 reduce-scatter.5.cloned.1.call-update
  218.9 0.0 reduce-scatter.7.cloned.1.call-start
  219.0 71.2 %reduce-scatter.5.cloned.1.call-done = bf16[128,640]{1,0:T(8,128)(2,1)} async-done(((bf16[2048,640]{1,0:T(8,128)(2,1)}), bf16[128,640]{1,0:T(8,128)(2,1)}) %reduce-scatter.5.cloned.1.call-update) | async-done | bytes 163856 | tf_op jit(solution)/shard_map/reduce_scatter | solution.py:57
  290.2 0.0 copy-done
  290.2 0.0 copy-done.2
  290.2 3.2 convolution_convert_fusion
  293.4 4.3 %copy.27 = bf16[2,128,2560]{1,0,2:T(2,128)(2,1)} copy(bf16[2,128,2560]{2,1,0:T(8,128)(2,1)} %convolution_convert_fusion) | data formatting | bytes 2621440
  297.7 0.0 copy-start.3
  297.7 2.6 copy.31
  300.3 0.0 reduce-scatter.7.cloned.1.call-update
  300.3 27.3 %reduce-scatter.7.cloned.1.call-done = bf16[640,256]{1,0:T(8,128)(2,1)} async-done(((bf16[2560,256]{1,0:T(8,128)(2,1)}), bf16[640,256]{1,0:T(8,128)(2,1)}) %reduce-scatter.7.cloned.1.call-update) | async-done | bytes 327696
  327.6 1.8 reshape.35
  329.4 1.9 copy.28
  331.3 1.9 fusion.14
  333.2 2.7 collective-permute-start
  336.0 0.0 copy-done.3
  336.0 12.7 %collective-permute-done = bf16[2,128,640]{2,1,0:T(8,128)(2,1)} collective-permute-done((bf16[2,128,640]{2,1,0:T(8,128)(2,1)}, bf16[2,128,640]{2,1,0:T(8,128)(2,1)}, u32[]{:S(2)}, u32[]{:S(2)}) %collective-permute-start) | collective-permute-done | bytes 327712 | tf_op jit(solution)/shard_map/ppermute | solution.py:15
  348.8 1.7 fusion.17
  (4 shorter events, 0.1 us)
Async XLA Ops:
  6.5 283.7 %copy-start = (bf16[1,2560,640]{2,1,0:T(8,128)(2,1)S(1)}, bf16[1,2560,640]{2,1,0:T(8,128)(2,1)}, u32[]{:S(2)}) copy-start(bf16[1,2560,640]{2,1,0:T(8,128)(2,1)} %param.13) | copy-start | bytes 9830404
  6.5 90.0 %all-gather.11.cloned.1.call-start = ((), (), s32[]{:S(2)}) async-start(), calls=%async_computation.5 | async-start | bytes 2785280 | tf_op jit(solution)/shard_map/all_gather | solution.py:45
  8.4 116.1 %all-gather.7.cloned.1.call-start = ((), (), s32[]{:S(2)}) async-start(), calls=%async_computation.3 | async-start | bytes 1638400 | tf_op jit(solution)/shard_map/all_gather | solution.py:35
  9.2 195.0 %all-gather.9.cloned.1.call-start = ((), (), s32[]{:S(2)}) async-start(), calls=%async_computation.4 | async-start | bytes 3481600 | tf_op jit(solution)/shard_map/all_gather | solution.py:37
  9.9 280.3 %reduce-scatter.5.cloned.1.call-start = ((), (), s32[]{:S(2)}) async-start(), calls=%async_computation.2 | async-start | bytes 2785280 | tf_op jit(solution)/shard_map/reduce_scatter | solution.py:57
  99.3 2.3 copy-start.1
  214.5 75.7 %copy-start.2 = (bf16[1,128,640]{2,1,0:T(8,128)(2,1)S(1)}, bf16[1,128,640]{2,1,0:T(8,128)(2,1)}, u32[]{:S(2)}) copy-start(bf16[1,128,640]{2,1,0:T(8,128)(2,1)} %get-tuple-element.6) | copy-start | bytes 491524
  218.9 108.7 %reduce-scatter.7.cloned.1.call-start = ((), (), s32[]{:S(2)}) async-start(), calls=%async_computation.6 | async-start | bytes 1638400
  297.7 38.3 %copy-start.3 = (bf16[128,640]{1,0:T(8,128)(2,1)S(1)}, bf16[128,640]{1,0:T(8,128)(2,1)}, u32[]{:S(2)}) copy-start(bf16[128,640]{1,0:T(8,128)(2,1)} %param.10) | copy-start | bytes 491524
  333.2 15.6 %collective-permute-start = (bf16[2,128,640]{2,1,0:T(8,128)(2,1)}, bf16[2,128,640]{2,1,0:T(8,128)(2,1)}, u32[]{:S(2)}, u32[]{:S(2)}) collective-permute-start(bf16[2,128,640]{2,1,0:T(8,128)(2,1)} %fusion.14), channel_id=1, source_target_pairs={{64,0},{128,64},{192,128},{256,192},{320,256},{384,320},{448,384},... | collective-permute-start | bytes 983048 | tf_op jit(solution)/shard_map/ppermute | solution.py:15
Sparse Core Ops, SparseCore 0:
  9.4 87.1 all-gather.10
  98.7 25.7 all-gather.6
  126.6 77.5 all-gather.8
  219.1 71.0 reduce-scatter.4
  300.4 27.1 reduce-scatter.6
where the time goes:
time: 358 us; the launch traced here: 357 us
  waiting for transfers between devices  297 us (83%)
  local copies, waits for them, and re-layouts  21.7 us (6%)
  matrix products  14.7 us (4%)
  between operations  13.9 us (4%)
  other arithmetic  6.49 us (2%)
    all_gather x1, waiting for transfers between devices, shards(): key_all = lax.all_gather(saved_keys[0], 'tok', axis=0, tiled=True)  83 us
    all_gather x1, waiting for transfers between devices, shards(): out_full = lax.all_gather(out_weight[0], 'tok', axis=0, tiled=True)  79.6 us
    reduce_scatter x1, waiting for transfers between devices, shards(): lax.psum_scatter(terms.reshape(lax.axis_size('tok') * rows_here, groups_h...  71.2 us
    unnamed x6, waiting for transfers between devices  28.7 us
    all_gather x1, waiting for transfers between devices, shards(): whole_cot = lax.all_gather(held_cotangents[0], 'head', axis=2, tiled=True)  21.9 us
    unnamed x14, local copies, waits for them, and re-layouts  15.8 us
    ppermute x1, waiting for transfers between devices, shifted(): lax.ppermute(value, axis, [(source, source + steps) for source in range(l...  12.7 us
  transfers between devices with their start and end apart: 6, of which 6 were waited for; matrix products, arithmetic and copies ran while one was open for 2% of the time, Pallas kernels for 0%

commit v1 on v0

v1 whole, which is shorter than its diff:
```python
import functools

import jax
import jax.numpy as jnp
from jax import lax
from jax.experimental import pallas as pl
from jax.experimental.pallas import tpu as pltpu
from jax.sharding import PartitionSpec as P

HD = 128
GUIDE = 3.0
MESH = pl.DeviceIdType.MESH
LOG2E = 1.4426950408889634
NT = (((1,), (1,)), ((), ()))
QCHUNK = 256


def kernel(
    n_sec,
    n_head,
    n_tok,
    held,
    qs,
    ks,
    vw,
    ow,
    bgate,
    tgate,
    tstep,
    out,
    held_v,
    scaled,
    w_full,
    v_full,
    q_all,
    k_all,
    g_all,
    probs,
    grad,
    o_buf,
    vgrad,
    part,
    part_in,
    cot,
    load_sem,
    a_send,
    a_recv,
    r_send,
    r_recv,
    q_send,
    q_recv,
    k_send,
    k_recv,
    g_send,
    g_recv,
    o_send,
    o_recv,
    p_send,
    p_recv,
    c_send,
    c_recv,
):
    sec, head, z = lax.axis_index("section"), lax.axis_index("head"), lax.axis_index("tok")
    core = lax.rem(head, 2)
    width = held.shape[3]
    rows = held.shape[2]
    heads_here = width // HD
    wrows = ow.shape[1]
    half_rows = wrows // 2
    right, left = lax.rem(z + 1, n_tok), lax.rem(z + n_tok - 1, n_tok)
    my_head = z // 3
    owner = jnp.logical_and(lax.rem(z, 3) == core, z < 3 * heads_here)

    def wblock(index, half):
        start = pl.multiple_of(index * wrows + half * half_rows, 16)
        return w_full.at[pl.ds(start, half_rows), :]

    load_held = pltpu.make_async_copy(held.at[0], held_v, load_sem.at[0])
    load_held.start()
    load_w = pltpu.make_async_copy(
        ow.at[0], w_full.at[pl.ds(pl.multiple_of(z * wrows, 16), wrows), :], load_sem.at[1]
    )
    load_w.start()
    load_v = pltpu.make_async_copy(vw.at[0], v_full, load_sem.at[2])
    load_v.start()

    barrier = pltpu.get_barrier_semaphore()
    for step in range(1, n_tok):
        pl.semaphore_signal(
            barrier, inc=1, device_id={"tok": lax.rem(z + step, n_tok)}, device_id_type=MESH
        )
    for step in range(1, n_head):
        pl.semaphore_signal(
            barrier, inc=1, device_id={"head": lax.rem(head + step, n_head)}, device_id_type=MESH
        )
    for step in (1, n_sec - 1):
        pl.semaphore_signal(
            barrier, inc=1, device_id={"section": lax.rem(sec + step, n_sec)}, device_id_type=MESH
        )
    pl.semaphore_wait(barrier, n_tok - 1 + n_head - 1 + 2)

    def ring(direction, half, step):
        block = lax.rem(z + n_tok - step, n_tok) if direction == 0 else lax.rem(z + step, n_tok)
        view = wblock(block, half)
        return pltpu.make_async_remote_copy(
            src_ref=view,
            dst_ref=view,
            send_sem=r_send.at[direction, half, step],
            recv_sem=r_recv.at[direction, half, step],
            device_id={"tok": right if direction == 0 else left},
            device_id_type=MESH,
        )

    load_w.wait()
    for half in (0, 1):
        for direction in (0, 1):
            ring(direction, half, 0).start()

    time_row = jnp.sum(
        jnp.where(
            lax.broadcasted_iota(jnp.int32, (tgate.shape[0], width), 0) == tstep[0],
            tgate[:, pl.ds(pl.multiple_of(head * width, 128), width)],
            0.0,
        ),
        axis=0,
        keepdims=True,
    )
    gate_row = bgate[:, pl.ds(pl.multiple_of(head * width, 128), width)] + time_row
    load_held.wait()
    for branch in (0, 1):
        scaled[head, branch * rows : (branch + 1) * rows, :] = (
            held_v[branch].astype(jnp.float32) * gate_row
        ).astype(jnp.bfloat16)

    def to_mate(step):
        return pltpu.make_async_remote_copy(
            src_ref=scaled.at[head],
            dst_ref=scaled.at[head],
            send_sem=a_send.at[step - 1],
            recv_sem=a_recv.at[step - 1],
            device_id={"head": lax.rem(head + step, n_head)},
            device_id_type=MESH,
        )

    for step in range(1, n_head):
        to_mate(step).start()

    def to_owner(source, target_ref, send_sem, recv_sem, index):
        owner_z = 3 * index + core

        @pl.when(owner_z == z)
        def _():
            pltpu.make_async_copy(source, target_ref.at[z], recv_sem).start()

        @pl.when(owner_z != z)
        def _():
            pltpu.make_async_remote_copy(
                src_ref=source,
                dst_ref=target_ref.at[z],
                send_sem=send_sem.at[index],
                recv_sem=recv_sem,
                device_id={"tok": owner_z},
                device_id_type=MESH,
            ).start()

    def wait_to_owner(source, target_ref, send_sem, recv_sem, index):
        owner_z = 3 * index + core

        @pl.when(owner_z != z)
        def _():
            pltpu.make_async_remote_copy(
                src_ref=source,
                dst_ref=target_ref.at[z],
                send_sem=send_sem.at[index],
                recv_sem=recv_sem,
                device_id={"tok": owner_z},
                device_id_type=MESH,
            ).wait_send()

    def head_cols(index):
        return slice(index * HD, (index + 1) * HD)

    for index in range(heads_here):
        to_owner(ks.at[0, :, head_cols(index)], k_all, k_send, k_recv, index)
        to_owner(qs.at[0, :, head_cols(index)], q_all, q_send, q_recv, index)

    chunks = n_tok * rows // QCHUNK
    per_chunk = QCHUNK // rows

    def weigh(chunk):
        query = q_all[pl.ds(chunk * per_chunk, per_chunk)].reshape(QCHUNK, HD)
        key = k_all[...].reshape(n_tok * rows, HD)
        raw = lax.dot_general(key, query, NT, preferred_element_type=jnp.float32) * (
            HD ** (-0.5) * LOG2E
        )
        top = jnp.max(raw, axis=0, keepdims=True)
        grown = jnp.exp2(raw - top)
        total = jnp.sum(grown, axis=0, keepdims=True)
        cols = pl.ds(pl.multiple_of(chunk * QCHUNK, QCHUNK), QCHUNK)
        probs[:, cols] = (grown * (1.0 / total)).astype(jnp.bfloat16)

    last = n_tok // 2 - 1
    first_weigh = last - chunks // 2 + 1

    def hop(step, sends):
        for half in (0, 1):
            for direction in (0, 1):
                ring(direction, half, step - 1).wait_recv()
                if (direction, half) in sends:
                    ring(direction, half, step).start()

    def weigh_at(step):
        @pl.when(jnp.logical_and(owner, step >= first_weigh))
        def _():
            @pl.when(step == first_weigh)
            def _():
                pltpu.make_async_copy(k_all, k_all, k_recv).wait()
                pltpu.make_async_copy(q_all, q_all, q_recv).wait()

            @pl.loop(0, 2)
            def _(turn):
                weigh((step - first_weigh) * 2 + turn)

    @pl.loop(1, last)
    def _(step):
        hop(step, ((0, 0), (0, 1), (1, 0), (1, 1)))
        weigh_at(step)

    hop(last, ((0, 0), (1, 1)))
    weigh_at(jnp.int32(last))
    for step in range(1, n_head):
        to_mate(step).wait_recv()
    ring(0, 0, last).wait_recv()
    ring(1, 1, last).wait_recv()

    for low in range(0, width, 2 * HD):
        high = min(low + 2 * HD, width)
        total = None
        for part_head in range(n_head):
            term = jnp.dot(
                scaled[part_head],
                w_full[part_head * width : (part_head + 1) * width, low:high],
                preferred_element_type=jnp.float32,
            )
            total = term if total is None else total + term
        for branch in (0, 1):
            grad[branch, :, low:high] = total[branch * rows : (branch + 1) * rows].astype(jnp.bfloat16)
        for index in range(low // HD, high // HD):
            to_owner(grad.at[0, :, head_cols(index)], g_all, g_send, g_recv, index)

    load_v.wait()

    def piece(branch, step):
        return pltpu.make_async_remote_copy(
            src_ref=part.at[branch, step],
            dst_ref=part_in.at[branch, step - 1],
            send_sem=p_send.at[branch, step - 1],
            recv_sem=p_recv.at[branch, step - 1],
            device_id={"head": lax.rem(head + step, n_head)},
            device_id_type=MESH,
        )

    def project(branch, value):
        for step in (2, 1, 3, 0):
            target = lax.rem(head + step, n_head)
            weight = v_full[pl.ds(pl.multiple_of(target * width, 128), width), :]
            part[branch, step] = lax.dot_general(
                value, weight, NT, preferred_element_type=jnp.float32
            ).astype(jnp.bfloat16)
            if step:
                piece(branch, step).start()

    def relay(branch):
        return pltpu.make_async_remote_copy(
            src_ref=cot.at[branch],
            dst_ref=out.at[branch],
            send_sem=c_send.at[branch],
            recv_sem=c_recv.at[branch],
            device_id={"section": lax.rem(sec + n_sec - 1, n_sec)},
            device_id_type=MESH,
        )

    def finish(branch):
        for step in range(1, n_head):
            piece(branch, step).wait_recv()
        back = part[branch, 0].astype(jnp.float32)
        for step in range(1, n_head):
            back = back + part_in[branch, step - 1].astype(jnp.float32)
        cot[branch] = (held_v[branch].astype(jnp.float32) + back).astype(jnp.bfloat16)
        relay(branch).start()

    project(1, grad[1])

    own_cols = pl.ds(pl.multiple_of(my_head * HD, HD), HD)

    def back_to(block):
        return pltpu.make_async_remote_copy(
            src_ref=o_buf.at[block],
            dst_ref=vgrad.at[:, own_cols],
            send_sem=o_send.at[block],
            recv_sem=o_recv,
            device_id={"tok": block},
            device_id_type=MESH,
        )

    @pl.when(owner)
    def _():
        pltpu.make_async_copy(g_all, g_all, g_recv).wait()

        @pl.loop(0, n_tok)
        def _(turn):
            block = lax.rem(z + n_tok // 2 + turn, n_tok)
            o_buf[block] = jnp.dot(
                probs[pl.ds(pl.multiple_of(block * rows, rows), rows), :],
                g_all[...].reshape(n_tok * rows, HD),
                preferred_element_type=jnp.float32,
            ).astype(jnp.bfloat16)

            @pl.when(block == z)
            def _():
                pltpu.make_async_copy(o_buf.at[block], vgrad.at[:, own_cols], o_recv).start()

            @pl.when(block != z)
            def _():
                back_to(block).start()

    finish(1)
    pltpu.make_async_copy(vgrad, vgrad, o_recv).wait()
    project(0, vgrad[...])
    finish(0)

    for index in range(heads_here):
        wait_to_owner(ks.at[0, :, head_cols(index)], k_all, k_send, k_recv, index)
        wait_to_owner(qs.at[0, :, head_cols(index)], q_all, q_send, q_recv, index)
        wait_to_owner(grad.at[0, :, head_cols(index)], g_all, g_send, g_recv, index)

    @pl.loop(0, last)
    def _(step):
        for half in (0, 1):
            for direction in (0, 1):
                ring(direction, half, step).wait_send()

    ring(0, 0, last).wait_send()
    ring(1, 1, last).wait_send()

    @pl.when(owner)
    def _():
        @pl.loop(0, n_tok)
        def _(block):
            @pl.when(block != z)
            def _():
                back_to(block).wait_send()

    for step in range(1, n_head):
        to_mate(step).wait_send()
        piece(0, step).wait_send()
        piece(1, step).wait_send()
    for branch in (1, 0):
        relay(branch).wait()


def shards(
    sizes,
    held_cotangents,
    entering_adjoint,
    saved_queries,
    saved_keys,
    value_weight,
    out_weight,
    block_gate,
    time_gate,
    timestep,
):
    n_sec, n_head, n_tok = sizes
    _, branches, rows, width = held_cotangents.shape
    heads_here = width // HD
    model = block_gate.shape[1]
    tokens = n_tok * rows
    bf16 = jnp.bfloat16
    dma = pltpu.SemaphoreType.DMA
    anywhere = pl.BlockSpec(memory_space=pl.ANY)
    vmem = pl.BlockSpec(memory_space=pltpu.VMEM)
    passed_on = pl.pallas_call(
        functools.partial(kernel, n_sec, n_head, n_tok),
        out_shape=jax.ShapeDtypeStruct((branches, rows, width), bf16),
        in_specs=[anywhere] * 5 + [vmem, vmem, pl.BlockSpec(memory_space=pltpu.SMEM)],
        out_specs=anywhere,
        scratch_shapes=[
            pltpu.VMEM((branches, rows, width), bf16),
            pltpu.VMEM((n_head, branches * rows, width), bf16),
            pltpu.VMEM((model, width), bf16),
            pltpu.VMEM((model, width), bf16),
            pltpu.VMEM((n_tok, rows, HD), bf16),
            pltpu.VMEM((n_tok, rows, HD), bf16),
            pltpu.VMEM((n_tok, rows, HD), bf16),
            pltpu.VMEM((tokens, tokens), bf16),
            pltpu.VMEM((branches, rows, width), bf16),
            pltpu.VMEM((n_tok, rows, HD), bf16),
            pltpu.VMEM((rows, width), bf16),
            pltpu.VMEM((branches, n_head, rows, width), bf16),
            pltpu.VMEM((branches, n_head - 1, rows, width), bf16),
            pltpu.VMEM((branches, rows, width), bf16),
            dma((3,)),
            dma((n_head - 1,)),
            dma((n_head - 1,)),
            dma((2, 2, n_tok // 2)),
            dma((2, 2, n_tok // 2)),
            dma((heads_here,)),
            dma,
            dma((heads_here,)),
            dma,
            dma((heads_here,)),
            dma,
            dma((n_tok,)),
            dma,
            dma((branches, n_head - 1)),
            dma((branches, n_head - 1)),
            dma((branches,)),
            dma((branches,)),
        ],
        compiler_params=pltpu.CompilerParams(
            collective_id=0, has_side_effects=True, vmem_limit_bytes=56 * 1024 * 1024
        ),
        name="tick",
    )(
        held_cotangents,
        saved_queries,
        saved_keys,
        value_weight,
        out_weight,
        block_gate,
        time_gate,
        timestep,
    )
    entering_full = entering_adjoint.astype(jnp.float32)
    fresh_rows = jnp.stack([(1.0 + GUIDE) * entering_full, -GUIDE * entering_full]).astype(bf16)
    is_last = lax.axis_index("section") == n_sec - 1
    return jnp.where(is_last, fresh_rows, passed_on)[None]


def solution(mesh):
    sizes = (mesh.shape["section"], mesh.shape["head"], mesh.shape["tok"])
    return jax.shard_map(
        functools.partial(shards, sizes),
        mesh=mesh,
        in_specs=(
            P("section", None, "tok", "head"),
            P("tok", "head"),
            P("section", "tok", "head"),
            P("section", "tok", "head"),
            P("section", None, "head"),
            P("section", "tok", "head"),
            P("section", None),
            P(),
            P(),
        ),
        out_specs=P("section", None, "tok", "head"),
        check_vma=False,
    )
```

time: 358 us -> 118 us (0.33)
  the two profiles are of different devices: /device:TPU:6 before, /device:TPU:5 now
where the time goes in v1:
time: 118 us
  Pallas kernels  115 us (97%)
  other arithmetic  1.8 us (2%)
    pallas_call x1, Pallas kernels, shards(): pl.pallas_call(functools.partial(kernel, n_sec, n_head, n_tok), out_shape...  115 us

profile of v1, /device:TPU:5, one launch (start us, length us, event | category | flops | bytes accessed | tf_op | source)
XLA Modules:
  0.0 117.5 jit_solution(5926918514665561400)
XLA Ops:
  0.0 0.0 copy-start
  0.7 115.0 %tick.1 = bf16[2,128,640]{2,1,0:T(8,128)(2,1)} custom-call(bf16[1,2,128,640]{3,2,1,0:T(8,128)(2,1)} %held.1, bf16[1,128,640]{2,1,0:T(8,128)(2,1)} %qs.1, bf16[1,128,640]{2,1,0:T(8,128)(2,1)} %ks.1, bf16[1,2560,640]{2,1,0:T(8,128)(2,1)} %vw.1, bf16[1,160,640]{2,1,0:T(8,128)(2,1)} %ow.1, f32[1,2560]{1,0:T(1,128)} %bgate.1, f32[32,2560]{1,0:T(8,128)} %tgate.1, ...), custom_call_target="tpu_custom_call" | custom-call | tf_op jit(solution)/shard_map/tick/pallas_call | solution.py:383
  115.7 0.0 copy-done
  115.8 1.8 %fusion.2 = bf16[1,2,128,640]{3,2,1,0:T(8,128)(2,1)} fusion(bf16[2,128,640]{2,1,0:T(8,128)(2,1)} %tick.1, bf16[1,128,640]{2,1,0:T(8,128)(2,1)S(1)} %get-tuple-element.6, bf16[1,128,640]{2,1,0:T(8,128)(2,1)S(1)} %get-tuple-element.5, pred[]{:T(512)S(6)} %eq.3), kind=kLoop, calls=%fused_computation.5 | loop fusion | flops 327680 | bytes 983041 | tf_op jit(solution)/shard_map/broadcast_in_dim | solution.py:438
  (1 shorter events, 0.0 us)
Async XLA Ops:
  0.0 115.7 %copy-start = (bf16[128,640]{1,0:T(8,128)(2,1)S(1)}, bf16[128,640]{1,0:T(8,128)(2,1)}, u32[]{:S(2)}) copy-start(bf16[128,640]{1,0:T(8,128)(2,1)} %param.10) | copy-start | bytes 491524

commit v2 on v1

v2 whole, which is shorter than its diff:
```python
import functools

import jax
import jax.numpy as jnp
from jax import lax
from jax.experimental import pallas as pl
from jax.experimental.pallas import tpu as pltpu
from jax.sharding import PartitionSpec as P

HD = 128
GUIDE = 3.0
MESH = pl.DeviceIdType.MESH
LOG2E = 1.4426950408889634
NT = (((1,), (1,)), ((), ()))
QCHUNK = 256
PIECES = 5
K_AT = 1
Q_AT = 1
WEIGH_AT = 4
PER_STEP = 2


def kernel(
    n_sec,
    n_head,
    n_tok,
    held,
    qs,
    ks,
    vw,
    ow,
    bgate,
    tgate,
    tstep,
    out,
    held_v,
    scaled,
    w_full,
    v_full,
    q_all,
    k_all,
    g_all,
    probs,
    grad,
    o_buf,
    vgrad,
    part,
    part_in,
    own,
    pair,
    pair_in,
    held_next,
    load_sem,
    a_send,
    a_recv,
    r_send,
    r_recv,
    q_send,
    q_recv,
    k_send,
    k_recv,
    g_send,
    g_recv,
    o_send,
    o_recv,
    p_send,
    p_recv,
    c_send,
    c_recv,
):
    sec, head, z = lax.axis_index("section"), lax.axis_index("head"), lax.axis_index("tok")
    core = lax.rem(head, 2)
    width = held.shape[3]
    rows = held.shape[2]
    heads_here = width // HD
    wrows = ow.shape[1]
    piece_rows = wrows // PIECES
    hops = n_tok // 2
    half = rows // 2
    mate = head + 1 - 2 * core
    row_y = head // 2
    right, left = lax.rem(z + 1, n_tok), lax.rem(z + n_tok - 1, n_tok)
    my_head = z // 3
    owner = jnp.logical_and(lax.rem(z, 3) == core, z < 3 * heads_here)

    load_held = pltpu.make_async_copy(held.at[0], held_v, load_sem.at[0])
    load_held.start()
    load_w = pltpu.make_async_copy(
        ow.at[0], w_full.at[pl.ds(pl.multiple_of(z * wrows, 16), wrows), :], load_sem.at[1]
    )
    load_w.start()
    load_v = pltpu.make_async_copy(vw.at[0], v_full, load_sem.at[2])
    load_v.start()

    barrier = pltpu.get_barrier_semaphore()
    for step in range(1, n_tok):
        pl.semaphore_signal(
            barrier, inc=1, device_id={"tok": lax.rem(z + step, n_tok)}, device_id_type=MESH
        )
    for step in range(1, n_head):
        pl.semaphore_signal(
            barrier, inc=1, device_id={"head": lax.rem(head + step, n_head)}, device_id_type=MESH
        )
    for step in (1, n_sec - 1):
        for turn in (0, 2):
            pl.semaphore_signal(
                barrier,
                inc=1,
                device_id={
                    "section": lax.rem(sec + step, n_sec),
                    "head": lax.rem(head + turn, n_head),
                },
                device_id_type=MESH,
            )
    pl.semaphore_wait(barrier, n_tok - 1 + n_head - 1 + 4)

    def ring(direction, index, step):
        block = lax.rem(z + n_tok - step, n_tok) if direction == 0 else lax.rem(z + step, n_tok)
        start = pl.multiple_of(block * wrows + index * piece_rows, 16)
        view = w_full.at[pl.ds(start, piece_rows), :]
        return pltpu.make_async_remote_copy(
            src_ref=view,
            dst_ref=view,
            send_sem=r_send.at[direction, index, step],
            recv_sem=r_recv.at[direction, index, step],
            device_id={"tok": right if direction == 0 else left},
            device_id_type=MESH,
        )

    def reach(direction, index):
        return hops - (direction + index) % 2

    load_w.wait()
    for index in range(PIECES):
        for direction in (0, 1):
            ring(direction, index, 0).start()

    time_row = jnp.sum(
        jnp.where(
            lax.broadcasted_iota(jnp.int32, (tgate.shape[0], width), 0) == tstep[0],
            tgate[:, pl.ds(pl.multiple_of(head * width, 128), width)],
            0.0,
        ),
        axis=0,
        keepdims=True,
    )
    gate_row = bgate[:, pl.ds(pl.multiple_of(head * width, 128), width)] + time_row
    load_held.wait()
    for branch in (0, 1):
        scaled[head, branch * rows : (branch + 1) * rows, :] = (
            held_v[branch].astype(jnp.float32) * gate_row
        ).astype(jnp.bfloat16)

    def to_mate(step):
        return pltpu.make_async_remote_copy(
            src_ref=scaled.at[head],
            dst_ref=scaled.at[head],
            send_sem=a_send.at[step - 1],
            recv_sem=a_recv.at[step - 1],
            device_id={"head": lax.rem(head + step, n_head)},
            device_id_type=MESH,
        )

    for step in range(1, n_head):
        to_mate(step).start()

    def hand_down(source, target, send_sem, recv_sem, head_index):
        return pltpu.make_async_remote_copy(
            src_ref=source,
            dst_ref=target,
            send_sem=send_sem,
            recv_sem=recv_sem,
            device_id={"section": lax.rem(sec + n_sec - 1, n_sec), "head": head_index},
            device_id_type=MESH,
        )

    def held_copy():
        return hand_down(held_v, held_next, c_send.at[0], c_recv.at[0], head)

    sends_down = sec > 0
    takes_down = sec < n_sec - 1
    pl.when(sends_down)(lambda: held_copy().start())

    def to_owner(source, target_ref, send_sem, recv_sem, index):
        owner_z = 3 * index + core

        @pl.when(owner_z == z)
        def _():
            pltpu.make_async_copy(source, target_ref.at[z], recv_sem).start()

        @pl.when(owner_z != z)
        def _():
            pltpu.make_async_remote_copy(
                src_ref=source,
                dst_ref=target_ref.at[z],
                send_sem=send_sem.at[index],
                recv_sem=recv_sem,
                device_id={"tok": owner_z},
                device_id_type=MESH,
            ).start()

    def wait_to_owner(source, target_ref, send_sem, recv_sem, index):
        owner_z = 3 * index + core

        @pl.when(owner_z != z)
        def _():
            pltpu.make_async_remote_copy(
                src_ref=source,
                dst_ref=target_ref.at[z],
                send_sem=send_sem.at[index],
                recv_sem=recv_sem,
                device_id={"tok": owner_z},
                device_id_type=MESH,
            ).wait_send()

    def head_cols(index):
        return slice(index * HD, (index + 1) * HD)

    def key_part(side, index):
        return ks.at[0, side * half : (side + 1) * half, head_cols(index)]

    def send_keys():
        for index in range(heads_here):
            for side in (0, 1):
                to_owner(key_part(side, index), k_all.at[side], k_send.at[side], k_recv, index)

    def send_queries():
        for index in range(heads_here):
            to_owner(qs.at[0, :, head_cols(index)], q_all, q_send, q_recv.at[z], index)

    chunks = n_tok * rows // QCHUNK
    per_chunk = QCHUNK // rows

    def weigh(chunk):
        query = q_all[pl.ds(chunk * per_chunk, per_chunk)].reshape(QCHUNK, HD)
        key = k_all[...].reshape(n_tok * rows, HD)
        raw = lax.dot_general(key, query, NT, preferred_element_type=jnp.float32) * (
            HD ** (-0.5) * LOG2E
        )
        top = jnp.max(raw, axis=0, keepdims=True)
        grown = jnp.exp2(raw - top)
        total = jnp.sum(grown, axis=0, keepdims=True)
        cols = pl.ds(pl.multiple_of(chunk * QCHUNK, QCHUNK), QCHUNK)
        probs[:, cols] = (grown * (1.0 / total)).astype(jnp.bfloat16)

    def advance(step):
        for index in range(PIECES):
            for direction in (0, 1):
                count = reach(direction, index)

                @pl.when(step <= count)
                def _():
                    ring(direction, index, step - 1).wait_recv()

                @pl.when(step < count)
                def _():
                    ring(direction, index, step).start()

    def weigh_turn(turn):
        @pl.when(turn == 0)
        def _():
            pltpu.make_async_copy(k_all, k_all, k_recv).wait()

        shift = (turn + 1) // 2 * (2 * lax.rem(turn, 2) - 1)
        chunk = lax.rem(z // per_chunk + shift + chunks, chunks)
        for place in range(per_chunk):
            source = chunk * per_chunk + place
            view = q_all.at[source]
            pltpu.make_async_copy(view, view, q_recv.at[source]).wait()
        weigh(chunk)

    weighed = min(chunks, PER_STEP * (hops - WEIGH_AT))

    @pl.loop(1, hops + 1)
    def _(step):
        @pl.when(step == K_AT)
        def _():
            send_keys()

        @pl.when(step == Q_AT)
        def _():
            send_queries()

        advance(step)

        @pl.when(jnp.logical_and(owner, jnp.logical_and(step >= WEIGH_AT, step < hops)))
        def _():
            first = (step - WEIGH_AT) * PER_STEP

            @pl.loop(0, PER_STEP)
            def _(turn):
                pl.when(first + turn < weighed)(lambda: weigh_turn(first + turn))

    for step in range(1, n_head):
        to_mate(step).wait_recv()

    for low in range(0, width, 2 * HD):
        high = min(low + 2 * HD, width)
        total = None
        for part_head in range(n_head):
            term = jnp.dot(
                scaled[part_head],
                w_full[part_head * width : (part_head + 1) * width, low:high],
                preferred_element_type=jnp.float32,
            )
            total = term if total is None else total + term
        for branch in (0, 1):
            grad[branch, :, low:high] = total[branch * rows : (branch + 1) * rows].astype(jnp.bfloat16)
        for index in range(low // HD, high // HD):
            to_owner(grad.at[0, :, head_cols(index)], g_all, g_send, g_recv, index)

    load_v.wait()

    def exchange(branch, side):
        return pltpu.make_async_remote_copy(
            src_ref=part.at[branch, side],
            dst_ref=part_in.at[branch, side],
            send_sem=p_send.at[branch, side],
            recv_sem=p_recv.at[branch, side],
            device_id={"head": mate},
            device_id_type=MESH,
        )

    def pair_down(branch, side, y):
        slot = (branch * 2 + side) * 2
        return hand_down(
            pair.at[branch, side, y],
            pair_in.at[branch, side, row_y],
            c_send.at[1 + slot + y],
            c_recv.at[1 + slot + row_y],
            2 * y + core,
        )

    def project(branch, side, value):
        def back(target):
            weight = v_full[pl.ds(pl.multiple_of(target * width, 128), width), :]
            return lax.dot_general(value, weight, NT, preferred_element_type=jnp.float32)

        for y in range(n_head // 2):
            part[branch, side, y] = back(2 * y + 1 - core).astype(jnp.bfloat16)
        exchange(branch, side).start()
        for y in range(n_head // 2):
            own[y] = back(2 * y + core)
        exchange(branch, side).wait_recv()
        for y in range(n_head // 2):
            total = own[y] + part_in[branch, side, y].astype(jnp.float32)
            pair[branch, side, y] = total.astype(jnp.bfloat16)
            pl.when(sends_down)(lambda: pair_down(branch, side, y).start())

    def collect(branch, side):
        @pl.when(takes_down)
        def _():
            for y in range(n_head // 2):
                slot = (branch * 2 + side) * 2 + y
                view = pair_in.at[branch, side, y]
                pltpu.make_async_copy(view, view, c_recv.at[1 + slot]).wait()
            span = slice(side * half, (side + 1) * half)
            total = held_next[branch, span, :].astype(jnp.float32)
            for y in range(n_head // 2):
                total = total + pair_in[branch, side, y].astype(jnp.float32)
            out[branch, span, :] = total.astype(jnp.bfloat16)

    own_cols = pl.ds(pl.multiple_of(my_head * HD, HD), HD)

    def back_to(side, block):
        return pltpu.make_async_remote_copy(
            src_ref=o_buf.at[side, block],
            dst_ref=vgrad.at[side, :, own_cols],
            send_sem=o_send.at[side, block],
            recv_sem=o_recv.at[side],
            device_id={"tok": block},
            device_id_type=MESH,
        )

    for side in (0, 1):
        project(1, side, grad[1, side * half : (side + 1) * half, :])

    together = 2 * rows // half

    @pl.when(owner)
    def _():
        @pl.loop(weighed, chunks)
        def _(turn):
            weigh_turn(turn)

        pltpu.make_async_copy(g_all, g_all, g_recv).wait()
        groups = n_tok // together

        for side in (0, 1):

            @pl.loop(0, groups)
            def _(turn):
                base = lax.rem(z // together + groups // 2 + turn, groups) * together
                start = pl.multiple_of((side * n_tok + base) * half, together * half)
                several = jnp.dot(
                    probs[pl.ds(start, together * half), :],
                    g_all[...].reshape(n_tok * rows, HD),
                    preferred_element_type=jnp.float32,
                ).astype(jnp.bfloat16)
                for place in range(together):
                    block = base + place
                    o_buf[side, block] = several[place * half : (place + 1) * half]

                    @pl.when(block == z)
                    def _():
                        pltpu.make_async_copy(
                            o_buf.at[side, block], vgrad.at[side, :, own_cols], o_recv.at[side]
                        ).start()

                    @pl.when(block != z)
                    def _():
                        back_to(side, block).start()

    @pl.when(takes_down)
    def _():
        pltpu.make_async_copy(held_next, held_next, c_recv.at[0]).wait()

    @pl.when(jnp.logical_not(takes_down))
    def _():
        out[...] = jnp.zeros_like(out)

    for side in (0, 1):
        collect(1, side)
    for side in (0, 1):
        pltpu.make_async_copy(vgrad.at[side], vgrad.at[side], o_recv.at[side]).wait()
        project(0, side, vgrad[side])
    for side in (0, 1):
        collect(0, side)

    for index in range(heads_here):
        for side in (0, 1):
            wait_to_owner(key_part(side, index), k_all.at[side], k_send.at[side], k_recv, index)
        wait_to_owner(qs.at[0, :, head_cols(index)], q_all, q_send, q_recv.at[z], index)
        wait_to_owner(grad.at[0, :, head_cols(index)], g_all, g_send, g_recv, index)

    for index in range(PIECES):
        for direction in (0, 1):

            @pl.loop(0, reach(direction, index))
            def _(step):
                ring(direction, index, step).wait_send()

    @pl.when(owner)
    def _():
        for side in (0, 1):

            @pl.loop(0, n_tok)
            def _(block):
                @pl.when(block != z)
                def _():
                    back_to(side, block).wait_send()

    for step in range(1, n_head):
        to_mate(step).wait_send()
    for branch in (0, 1):
        for side in (0, 1):
            exchange(branch, side).wait_send()

    @pl.when(sends_down)
    def _():
        held_copy().wait_send()
        for branch in (0, 1):
            for side in (0, 1):
                for y in range(n_head // 2):
                    pair_down(branch, side, y).wait_send()


def shards(
    sizes,
    held_cotangents,
    entering_adjoint,
    saved_queries,
    saved_keys,
    value_weight,
    out_weight,
    block_gate,
    time_gate,
    timestep,
):
    n_sec, n_head, n_tok = sizes
    _, branches, rows, width = held_cotangents.shape
    heads_here = width // HD
    model = block_gate.shape[1]
    tokens = n_tok * rows
    bf16 = jnp.bfloat16
    dma = pltpu.SemaphoreType.DMA
    anywhere = pl.BlockSpec(memory_space=pl.ANY)
    vmem = pl.BlockSpec(memory_space=pltpu.VMEM)
    passed_on = pl.pallas_call(
        functools.partial(kernel, n_sec, n_head, n_tok),
        out_shape=jax.ShapeDtypeStruct((branches, rows, width), bf16),
        in_specs=[anywhere] * 5 + [vmem, vmem, pl.BlockSpec(memory_space=pltpu.SMEM)],
        out_specs=vmem,
        scratch_shapes=[
            pltpu.VMEM((branches, rows, width), bf16),
            pltpu.VMEM((n_head, branches * rows, width), bf16),
            pltpu.VMEM((model, width), bf16),
            pltpu.VMEM((model, width), bf16),
            pltpu.VMEM((n_tok, rows, HD), bf16),
            pltpu.VMEM((2, n_tok, rows // 2, HD), bf16),
            pltpu.VMEM((n_tok, rows, HD), bf16),
            pltpu.VMEM((tokens, tokens), bf16),
            pltpu.VMEM((branches, rows, width), bf16),
            pltpu.VMEM((2, n_tok, rows // 2, HD), bf16),
            pltpu.VMEM((2, rows // 2, width), bf16),
            pltpu.VMEM((branches, 2, n_head // 2, rows // 2, width), bf16),
            pltpu.VMEM((branches, 2, n_head // 2, rows // 2, width), bf16),
            pltpu.VMEM((n_head // 2, rows // 2, width), jnp.float32),
            pltpu.VMEM((branches, 2, n_head // 2, rows // 2, width), bf16),
            pltpu.VMEM((branches, 2, n_head // 2, rows // 2, width), bf16),
            pltpu.VMEM((branches, rows, width), bf16),
            dma((3,)),
            dma((n_head - 1,)),
            dma((n_head - 1,)),
            dma((2, PIECES, n_tok // 2)),
            dma((2, PIECES, n_tok // 2)),
            dma((heads_here,)),
            dma((n_tok,)),
            dma((2, heads_here)),
            dma,
            dma((heads_here,)),
            dma,
            dma((2, n_tok)),
            dma((2,)),
            dma((branches, 2)),
            dma((branches, 2)),
            dma((9,)),
            dma((9,)),
        ],
        compiler_params=pltpu.CompilerParams(
            collective_id=0, has_side_effects=True, vmem_limit_bytes=56 * 1024 * 1024
        ),
        name="tick",
    )(
        held_cotangents,
        saved_queries,
        saved_keys,
        value_weight,
        out_weight,
        block_gate,
        time_gate,
        timestep,
    )
    entering_full = entering_adjoint.astype(jnp.float32)
    fresh_rows = jnp.stack([(1.0 + GUIDE) * entering_full, -GUIDE * entering_full]).astype(bf16)
    is_last = lax.axis_index("section") == n_sec - 1
    return jnp.where(is_last, fresh_rows, passed_on)[None]


def solution(mesh):
    sizes = (mesh.shape["section"], mesh.shape["head"], mesh.shape["tok"])
    return jax.shard_map(
        functools.partial(shards, sizes),
        mesh=mesh,
        in_specs=(
            P("section", None, "tok", "head"),
            P("tok", "head"),
            P("section", "tok", "head"),
            P("section", "tok", "head"),
            P("section", None, "head"),
            P("section", "tok", "head"),
            P("section", None),
            P(),
            P(),
        ),
        out_specs=P("section", None, "tok", "head"),
        check_vma=False,
    )
```

time: 118 us -> 108 us (0.915)
  the two profiles are of different devices: /device:TPU:5 before, /device:TPU:6 now
where the time goes in v2:
time: 108 us
  Pallas kernels  105 us (97%)
  other arithmetic  1.8 us (2%)
    pallas_call x1, Pallas kernels, shards(): pl.pallas_call(functools.partial(kernel, n_sec, n_head, n_tok), out_shape...  105 us

profile of v2, /device:TPU:6, one launch (start us, length us, event | category | flops | bytes accessed | tf_op | source)
XLA Modules:
  0.0 107.8 jit_solution(7363815878856242252)
XLA Ops:
  0.0 0.0 copy-start
  0.7 105.2 %tick.1 = bf16[2,128,640]{2,1,0:T(8,128)(2,1)} custom-call(bf16[1,2,128,640]{3,2,1,0:T(8,128)(2,1)} %held.1, bf16[1,128,640]{2,1,0:T(8,128)(2,1)} %qs.1, bf16[1,128,640]{2,1,0:T(8,128)(2,1)} %ks.1, bf16[1,2560,640]{2,1,0:T(8,128)(2,1)} %vw.1, bf16[1,160,640]{2,1,0:T(8,128)(2,1)} %ow.1, f32[1,2560]{1,0:T(1,128)} %bgate.1, f32[32,2560]{1,0:T(8,128)} %tgate.1, ...), custom_call_target="tpu_custom_call" | custom-call | tf_op jit(solution)/shard_map/tick/pallas_call | solution.py:489
  105.9 0.0 copy-done
  106.0 1.8 %fusion.2 = bf16[1,2,128,640]{3,2,1,0:T(8,128)(2,1)} fusion(bf16[2,128,640]{2,1,0:T(8,128)(2,1)} %tick.1, bf16[1,128,640]{2,1,0:T(8,128)(2,1)S(1)} %get-tuple-element.6, bf16[1,128,640]{2,1,0:T(8,128)(2,1)S(1)} %get-tuple-element.5, pred[]{:T(512)S(6)} %eq.3), kind=kLoop, calls=%fused_computation.5 | loop fusion | flops 327680 | bytes 983041 | tf_op jit(solution)/shard_map/broadcast_in_dim | solution.py:547
  (1 shorter events, 0.0 us)
Async XLA Ops:
  0.0 105.9 %copy-start = (bf16[128,640]{1,0:T(8,128)(2,1)S(1)}, bf16[128,640]{1,0:T(8,128)(2,1)}, u32[]{:S(2)}) copy-start(bf16[128,640]{1,0:T(8,128)(2,1)} %param.10) | copy-start | bytes 491524

commit v3 on v2

--- a/solution.py
+++ b/solution.py
@@ -214,18 +214,23 @@
             ).wait_send()
 
     def head_cols(index):
-        return slice(index * HD, (index + 1) * HD)
+        return pl.ds(pl.multiple_of(index * HD, HD), HD)
+
+    turns = (2, 3, 1, 4, 0)
+
+    def spread(turn):
+        return lax.rem(z // 3 + turn, heads_here)
 
     def key_part(side, index):
         return ks.at[0, side * half : (side + 1) * half, head_cols(index)]
 
     def send_keys():
-        for index in range(heads_here):
+        for index in map(spread, turns):
             for side in (0, 1):
                 to_owner(key_part(side, index), k_all.at[side], k_send.at[side], k_recv, index)
 
     def send_queries():
-        for index in range(heads_here):
+        for index in map(spread, turns):
             to_owner(qs.at[0, :, head_cols(index)], q_all, q_send, q_recv.at[z], index)
 
     chunks = n_tok * rows // QCHUNK
@@ -294,20 +299,20 @@
     for step in range(1, n_head):
         to_mate(step).wait_recv()
 
-    for low in range(0, width, 2 * HD):
-        high = min(low + 2 * HD, width)
+    for index in map(spread, turns):
         total = None
-        for part_head in range(n_head):
+        for source in range(n_head):
             term = jnp.dot(
-                scaled[part_head],
-                w_full[part_head * width : (part_head + 1) * width, low:high],
+                scaled[source],
+                w_full[source * width : (source + 1) * width, head_cols(index)],
                 preferred_element_type=jnp.float32,
             )
             total = term if total is None else total + term
         for branch in (0, 1):
-            grad[branch, :, low:high] = total[branch * rows : (branch + 1) * rows].astype(jnp.bfloat16)
-        for index in range(low // HD, high // HD):
-            to_owner(grad.at[0, :, head_cols(index)], g_all, g_send, g_recv, index)
+            grad[branch, :, head_cols(index)] = total[branch * rows : (branch + 1) * rows].astype(
+                jnp.bfloat16
+            )
+        to_owner(grad.at[0, :, head_cols(index)], g_all, g_send, g_recv, index)
 
     load_v.wait()
 

time: 108 us -> 108 us (level)
  no operation moved by 1% of the time
where the time goes in v3:
time: 108 us; the launch traced here: 107 us
  Pallas kernels  105 us (97%)
  other arithmetic  1.8 us (2%)
    pallas_call x1, Pallas kernels, shards(): pl.pallas_call(functools.partial(kernel, n_sec, n_head, n_tok), out_shape...  105 us

profile of v3, /device:TPU:6, one launch (start us, length us, event | category | flops | bytes accessed | tf_op | source)
XLA Modules:
  0.0 107.4 jit_solution(8720044935692706320)
XLA Ops:
  0.0 0.0 copy-start
  0.7 104.8 %tick.1 = bf16[2,128,640]{2,1,0:T(8,128)(2,1)} custom-call(bf16[1,2,128,640]{3,2,1,0:T(8,128)(2,1)} %held.1, bf16[1,128,640]{2,1,0:T(8,128)(2,1)} %qs.1, bf16[1,128,640]{2,1,0:T(8,128)(2,1)} %ks.1, bf16[1,2560,640]{2,1,0:T(8,128)(2,1)} %vw.1, bf16[1,160,640]{2,1,0:T(8,128)(2,1)} %ow.1, f32[1,2560]{1,0:T(1,128)} %bgate.1, f32[32,2560]{1,0:T(8,128)} %tgate.1, ...), custom_call_target="tpu_custom_call" | custom-call | tf_op jit(solution)/shard_map/tick/pallas_call | solution.py:494
  105.5 0.0 copy-done
  105.6 1.8 %fusion.2 = bf16[1,2,128,640]{3,2,1,0:T(8,128)(2,1)} fusion(bf16[2,128,640]{2,1,0:T(8,128)(2,1)} %tick.1, bf16[1,128,640]{2,1,0:T(8,128)(2,1)S(1)} %get-tuple-element.6, bf16[1,128,640]{2,1,0:T(8,128)(2,1)S(1)} %get-tuple-element.5, pred[]{:T(512)S(6)} %eq.3), kind=kLoop, calls=%fused_computation.5 | loop fusion | flops 327680 | bytes 983041 | tf_op jit(solution)/shard_map/broadcast_in_dim | solution.py:552
  (1 shorter events, 0.0 us)
Async XLA Ops:
  0.0 105.5 %copy-start = (bf16[128,640]{1,0:T(8,128)(2,1)S(1)}, bf16[128,640]{1,0:T(8,128)(2,1)}, u32[]{:S(2)}) copy-start(bf16[128,640]{1,0:T(8,128)(2,1)} %param.10) | copy-start | bytes 491524

commit v4 on v3

--- a/solution.py
+++ b/solution.py
@@ -14,8 +14,8 @@
 NT = (((1,), (1,)), ((), ()))
 QCHUNK = 256
 PIECES = 5
-K_AT = 1
-Q_AT = 1
+K_AT = 2
+Q_AT = 2
 WEIGH_AT = 4
 PER_STEP = 2
 
@@ -239,11 +239,9 @@
     def weigh(chunk):
         query = q_all[pl.ds(chunk * per_chunk, per_chunk)].reshape(QCHUNK, HD)
         key = k_all[...].reshape(n_tok * rows, HD)
-        raw = lax.dot_general(key, query, NT, preferred_element_type=jnp.float32) * (
-            HD ** (-0.5) * LOG2E
-        )
+        raw = lax.dot_general(key, query, NT, preferred_element_type=jnp.float32)
         top = jnp.max(raw, axis=0, keepdims=True)
-        grown = jnp.exp2(raw - top)
+        grown = jnp.exp2((raw - top) * (HD ** (-0.5) * LOG2E))
         total = jnp.sum(grown, axis=0, keepdims=True)
         cols = pl.ds(pl.multiple_of(chunk * QCHUNK, QCHUNK), QCHUNK)
         probs[:, cols] = (grown * (1.0 / total)).astype(jnp.bfloat16)

time: 108 us -> 108 us (level)
  no operation moved by 1% of the time
where the time goes in v4:
time: 108 us
  Pallas kernels  105 us (97%)
  other arithmetic  1.8 us (2%)
    pallas_call x1, Pallas kernels, shards(): pl.pallas_call(functools.partial(kernel, n_sec, n_head, n_tok), out_shape...  105 us

profile of v4, /device:TPU:6, one launch (start us, length us, event | category | flops | bytes accessed | tf_op | source)
XLA Modules:
  0.0 107.6 jit_solution(9996590702476698752)
XLA Ops:
  0.0 0.0 copy-start
  0.7 105.1 %tick.1 = bf16[2,128,640]{2,1,0:T(8,128)(2,1)} custom-call(bf16[1,2,128,640]{3,2,1,0:T(8,128)(2,1)} %held.1, bf16[1,128,640]{2,1,0:T(8,128)(2,1)} %qs.1, bf16[1,128,640]{2,1,0:T(8,128)(2,1)} %ks.1, bf16[1,2560,640]{2,1,0:T(8,128)(2,1)} %vw.1, bf16[1,160,640]{2,1,0:T(8,128)(2,1)} %ow.1, f32[1,2560]{1,0:T(1,128)} %bgate.1, f32[32,2560]{1,0:T(8,128)} %tgate.1, ...), custom_call_target="tpu_custom_call" | custom-call | tf_op jit(solution)/shard_map/tick/pallas_call | solution.py:492
  105.8 0.0 copy-done
  105.9 1.8 %fusion.2 = bf16[1,2,128,640]{3,2,1,0:T(8,128)(2,1)} fusion(bf16[2,128,640]{2,1,0:T(8,128)(2,1)} %tick.1, bf16[1,128,640]{2,1,0:T(8,128)(2,1)S(1)} %get-tuple-element.6, bf16[1,128,640]{2,1,0:T(8,128)(2,1)S(1)} %get-tuple-element.5, pred[]{:T(512)S(6)} %eq.3), kind=kLoop, calls=%fused_computation.5 | loop fusion | flops 327680 | bytes 983041 | tf_op jit(solution)/shard_map/broadcast_in_dim | solution.py:550
  (1 shorter events, 0.0 us)
Async XLA Ops:
  0.0 105.8 %copy-start = (bf16[128,640]{1,0:T(8,128)(2,1)S(1)}, bf16[128,640]{1,0:T(8,128)(2,1)}, u32[]{:S(2)}) copy-start(bf16[128,640]{1,0:T(8,128)(2,1)} %param.10) | copy-start | bytes 491524

commit v5 on v3

--- a/solution.py
+++ b/solution.py
@@ -14,8 +14,9 @@
 NT = (((1,), (1,)), ((), ()))
 QCHUNK = 256
 PIECES = 5
-K_AT = 1
-Q_AT = 1
+K_AT = 2
+Q_AT = 2
+VOUCH_FIRST = 4
 WEIGH_AT = 4
 PER_STEP = 2
 
@@ -50,6 +51,7 @@
     pair,
     pair_in,
     held_next,
+    enter_sem,
     load_sem,
     a_send,
     a_recv,
@@ -93,10 +95,8 @@
     load_v.start()
 
     barrier = pltpu.get_barrier_semaphore()
-    for step in range(1, n_tok):
-        pl.semaphore_signal(
-            barrier, inc=1, device_id={"tok": lax.rem(z + step, n_tok)}, device_id_type=MESH
-        )
+    for neighbour in (left, right):
+        pl.semaphore_signal(barrier, inc=1, device_id={"tok": neighbour}, device_id_type=MESH)
     for step in range(1, n_head):
         pl.semaphore_signal(
             barrier, inc=1, device_id={"head": lax.rem(head + step, n_head)}, device_id_type=MESH
@@ -112,7 +112,17 @@
                 },
                 device_id_type=MESH,
             )
-    pl.semaphore_wait(barrier, n_tok - 1 + n_head - 1 + 4)
+    pl.semaphore_wait(barrier, 2 + n_head - 1 + 4)
+
+    def vouch(levels):
+        for _ in range(levels):
+            pl.semaphore_signal(
+                enter_sem.at[0], inc=1, device_id={"tok": right}, device_id_type=MESH
+            )
+            pl.semaphore_signal(enter_sem.at[1], inc=1, device_id={"tok": left}, device_id_type=MESH)
+            for side in (0, 1):
+                pl.semaphore_wait(enter_sem.at[side], 1)
+
 
     def ring(direction, index, step):
         block = lax.rem(z + n_tok - step, n_tok) if direction == 0 else lax.rem(z + step, n_tok)
@@ -276,10 +286,13 @@
 
     weighed = min(chunks, PER_STEP * (hops - WEIGH_AT))
 
+    vouch(VOUCH_FIRST)
+
     @pl.loop(1, hops + 1)
     def _(step):
         @pl.when(step == K_AT)
         def _():
+            vouch(hops - 1 - VOUCH_FIRST)
             send_keys()
 
         @pl.when(step == Q_AT)
@@ -514,6 +527,7 @@
             pltpu.VMEM((branches, 2, n_head // 2, rows // 2, width), bf16),
             pltpu.VMEM((branches, 2, n_head // 2, rows // 2, width), bf16),
             pltpu.VMEM((branches, rows, width), bf16),
+            pltpu.SemaphoreType.REGULAR((2,)),
             dma((3,)),
             dma((n_head - 1,)),
             dma((n_head - 1,)),

time: 108 us -> 107 us (level)
    pallas_call x1, Pallas kernels: 105 us -> 104 us  [shards(): pl.pallas_call(functools.partial(kernel, n_sec, n_head, n_tok), out_shape...]
where the time goes in v5:
time: 107 us; the launch traced here: 106 us
  Pallas kernels  104 us (97%)
  other arithmetic  1.8 us (2%)
    pallas_call x1, Pallas kernels, shards(): pl.pallas_call(functools.partial(kernel, n_sec, n_head, n_tok), out_shape...  104 us

profile of v5, /device:TPU:6, one launch (start us, length us, event | category | flops | bytes accessed | tf_op | source)
XLA Modules:
  0.0 106.2 jit_solution(6902804257197939064)
XLA Ops:
  0.0 0.0 copy-start
  0.7 103.7 %tick.1 = bf16[2,128,640]{2,1,0:T(8,128)(2,1)} custom-call(bf16[1,2,128,640]{3,2,1,0:T(8,128)(2,1)} %held.1, bf16[1,128,640]{2,1,0:T(8,128)(2,1)} %qs.1, bf16[1,128,640]{2,1,0:T(8,128)(2,1)} %ks.1, bf16[1,2560,640]{2,1,0:T(8,128)(2,1)} %vw.1, bf16[1,160,640]{2,1,0:T(8,128)(2,1)} %ow.1, f32[1,2560]{1,0:T(1,128)} %bgate.1, f32[32,2560]{1,0:T(8,128)} %tgate.1, ...), custom_call_target="tpu_custom_call" | custom-call | tf_op jit(solution)/shard_map/tick/pallas_call | solution.py:507
  104.4 0.0 copy-done
  104.5 1.8 %fusion.2 = bf16[1,2,128,640]{3,2,1,0:T(8,128)(2,1)} fusion(bf16[2,128,640]{2,1,0:T(8,128)(2,1)} %tick.1, bf16[1,128,640]{2,1,0:T(8,128)(2,1)S(1)} %get-tuple-element.6, bf16[1,128,640]{2,1,0:T(8,128)(2,1)S(1)} %get-tuple-element.5, pred[]{:T(512)S(6)} %eq.3), kind=kLoop, calls=%fused_computation.5 | loop fusion | flops 327680 | bytes 983041 | tf_op jit(solution)/shard_map/broadcast_in_dim | solution.py:566
  (1 shorter events, 0.0 us)
Async XLA Ops:
  0.0 104.4 %copy-start = (bf16[128,640]{1,0:T(8,128)(2,1)S(1)}, bf16[128,640]{1,0:T(8,128)(2,1)}, u32[]{:S(2)}) copy-start(bf16[128,640]{1,0:T(8,128)(2,1)} %param.10) | copy-start | bytes 491524
